TPU v7x, 32 devices: a whole 2x2x4 slice. The times are simulated.
32 devices in a mesh: rows: 2 (over x), cent: 16 (over z, y, core).
Axes of the slice: x: 2, y: 2, z: 4, core: 2. Of those that a mesh axis runs over, the one named last changes fastest.
Arguments:
- embeddings: bfloat16 [2048, 768], P(('rows', 'cent')), may hold values from -33 to 33
- centroids: bfloat16 [2048, 768], P('cent'), may hold values from -4 to 4
- group_length: int32 [2], P('rows'), may hold values from 256 to 1024, as said below
Outputs:
- new_centroids: bfloat16 [2048, 768], P('cent')
- new_moments: bfloat16 [2048, 768], P('cent')
- loglik: float32 [2048], P(('rows', 'cent'))
Inputs may be any that keep to these rules, and one draw needn't show every extreme that they name: Row group g uses its first group_length[g] of its 1024 row slots; at least one group uses all of them.
All inputs are finite; a program needn't handle non-finite values.
Results may differ from a plain program's by a relative error of at most 0.0047.
Values may be sent and summed in bfloat16 or wider, within the bound.
A program may use at most 64 MiB of HBM per device.

v0:
```python
import math
import jax
import jax.numpy as jnp
from jax import lax
from jax.sharding import PartitionSpec as P

score_factor = 3.0
prior_weight = 1.0
contract_rows = (((0,), (0,)), ((), ()))
contract_width = (((1,), (1,)), ((), ()))


def combined_all(part, axis, combine):
    gathered = jax.tree.map(lambda a: lax.all_gather(a, axis), part)

    def take(source):
        return jax.tree.map(lambda a: lax.dynamic_index_in_dim(a, source, 0, False), gathered)

    return lax.fori_loop(
        1, lax.axis_size(axis), lambda source, state: combine(state, take(source)), take(0)
    )


def scores(row_block, centroid_rows, squared_norm, factor):
    inner = lax.dot_general(
        row_block, centroid_rows, contract_width, preferred_element_type=jnp.float32
    )
    return factor * (inner - 0.5 * squared_norm[None, :])


def finish_totals(peaks, exp_sums):

    def combine(left_part, right_part):
        highest = jnp.maximum(left_part[0], right_part[0])
        joined = left_part[1] * jnp.exp(left_part[0] - highest) + right_part[1] * jnp.exp(
            right_part[0] - highest
        )
        return (highest, joined)

    peak_all, total_all = combined_all((peaks, exp_sums), "cent", combine)
    return peak_all + jnp.log(total_all)


def add_stats(row_piece, logits, piece_lse, valid_rows):
    responsibility = jnp.where(
        valid_rows[:, None], jnp.exp(logits - piece_lse[:, None]), 0.0
    ).astype(jnp.bfloat16)
    rows_wide = row_piece.astype(jnp.float32)
    squares = (rows_wide * rows_wide).astype(jnp.bfloat16)
    weighted = lax.dot_general(
        responsibility, row_piece, contract_rows, preferred_element_type=jnp.float32
    )
    moments = lax.dot_general(
        responsibility, squares, contract_rows, preferred_element_type=jnp.float32
    )
    weight_mass = jnp.sum(responsibility.astype(jnp.float32), axis=0)
    return (weighted, moments, weight_mass)


def shards(embeddings, centroids, group_length):
    row_count = embeddings.shape[0]
    width = embeddings.shape[1]
    factor = score_factor / math.sqrt(width)
    cent_wide = centroids.astype(jnp.float32)
    squared_norm = jnp.sum(cent_wide * cent_wide, axis=1)
    used_rows = group_length[0]
    offset = lax.axis_index("cent") * row_count
    own_positions = offset + jnp.arange(row_count, dtype=jnp.int32)
    own_valid = own_positions < used_rows
    logits = scores(
        lax.all_gather(embeddings, "cent", axis=0, tiled=True), centroids, squared_norm, factor
    )
    piece_peak = jnp.max(logits, axis=1)
    piece_total = jnp.sum(jnp.exp(logits - piece_peak[:, None]), axis=1)
    peaks = piece_peak
    exp_sums = piece_total
    peaks, exp_sums = (peaks, exp_sums)
    group_lse = finish_totals(peaks, exp_sums)
    row_piece = lax.all_gather(embeddings, "cent", axis=0, tiled=True)
    piece_count = row_piece.shape[0]
    logits = scores(row_piece, centroids, squared_norm, factor)
    positions = jnp.arange(piece_count, dtype=jnp.int32)
    weighted, moments, weight_mass = add_stats(row_piece, logits, group_lse, positions < used_rows)
    own_lse = lax.dynamic_slice_in_dim(group_lse, offset, row_count, 0)
    weighted, moments, weight_mass = lax.psum((weighted, moments, weight_mass), "rows")
    denominator = weight_mass[:, None] + prior_weight
    new_centroids = ((weighted + prior_weight * cent_wide) / denominator).astype(jnp.bfloat16)
    new_moments = ((moments + prior_weight) / denominator).astype(jnp.bfloat16)
    loglik = jnp.where(own_valid, own_lse, jnp.zeros_like(own_lse))
    return (new_centroids, new_moments, loglik)


def solution(mesh):
    return jax.shard_map(
        shards,
        mesh=mesh,
        in_specs=(P(("rows", "cent"), None), P("cent", None), P("rows")),
        out_specs=(P("cent", None), P("cent", None), P(("rows", "cent"))),
        check_vma=False,
    )
```

profile of v0, /device:TPU:0, one launch (start us, length us, event | category | flops | bytes accessed | tf_op | source)
XLA Modules:
  0.0 137.1 jit_solution(16626521679384497014)
XLA Ops:
  7.2 0.0 all-gather.4.cloned.1.call-start
  7.2 0.7 all-gather.4.cloned.1.call-update
  7.9 0.0 all-reduce.3.cloned.1.call-start
  8.6 1.0 fusion.2
  9.7 43.0 %all-gather.4.cloned.1.call-done = bf16[1024,768]{1,0:T(8,128)(2,1)} async-done(((bf16[64,768]{1,0:T(8,128)(2,1)}), bf16[1024,768]{1,0:T(8,128)(2,1)}) %all-gather.4.cloned.1.call-update) | async-done | bytes 1572880 | tf_op jit(solution)/shard_map/all_gather | solution.py:79
  52.6 2.1 %fusion.5 = (f32[1024]{0:T(1024)S(1)}, f32[1024,128]{0,1:T(8,128)S(1)}) fusion(f32[128]{0:T(128)S(1)} %broadcast_multiply_fusion, bf16[1024,768]{1,0:T(8,128)(2,1)} %all-gather.4.cloned.1.call-done, bf16[128,768]{1,0:T(8,128)(2,1)} %param.6), kind=kOutput, calls=%fused_computation.21 | convolution fusion | flops 201718784 | bytes 2298368 | tf_op jit(solution)/shard_map/dot_general | solution.py:25
  54.7 0.0 copy-start
  54.7 19.4 %all-gather = f32[16384]{0:T(1024)S(1)} all-gather(f32[1024]{0:T(1024)S(1)} %get-tuple-element.158), channel_id=2, replica_groups=mesh['rows'=2,'cent'=16] {'cent'}, dimensions={0}, use_global_device_ids=true | all-gather | bytes 69632 | tf_op jit(solution)/shard_map/all_gather | solution.py:14
  74.1 0.1 exponential_reduce_fusion
  74.2 17.6 %all-gather.1 = f32[16384]{0:T(1024)S(1)} all-gather(f32[1024]{0:T(1024)S(1)} %exponential_reduce_fusion), channel_id=3, replica_groups=mesh['rows'=2,'cent'=16] {'cent'}, dimensions={0}, use_global_device_ids=true | all-gather | bytes 69632 | tf_op jit(solution)/shard_map/all_gather | solution.py:14
  91.9 0.9 while.17
  92.8 0.2 convert_reduce_fusion
  93.0 0.0 copy-done
  93.0 1.2 fusion
  94.2 0.0 copy-start.1
  94.2 1.1 fusion.6
  95.3 0.0 all-reduce.3.cloned.1.call-update
  95.4 4.9 %psum.22 = f32[128]{0:T(128)S(1)} all-reduce(f32[128]{0:T(128)S(1)} %get-tuple-element.152), channel_id=1, replica_groups=mesh['rows'=2,'cent'=16] {'rows'}, use_global_device_ids=true, to_apply=%region_7.8 | all-reduce | flops 128 | bytes 1024 | tf_op jit(solution)/shard_map/psum | solution.py:85
  100.3 0.6 compare_select_fusion
  100.9 27.3 %all-reduce.3.cloned.1.call-done = (f32[128,768]{1,0:T(8,128)}, f32[128,768]{1,0:T(8,128)}) async-done(((f32[128,768]{1,0:T(8,128)}, f32[128,768]{1,0:T(8,128)}), (f32[128,768]{1,0:T(8,128)}, f32[128,768]{1,0:T(8,128)})) %all-reduce.3.cloned.1.call-update) | async-done | bytes 786448 | tf_op jit(solution)/shard_map/psum | solution.py:85
  128.2 0.0 copy-done.1
  128.2 2.0 %divide_convert_fusion = (bf16[128,768]{1,0:T(8,128)(2,1)}, bf16[128,768]{1,0:T(8,128)(2,1)}) fusion(f32[128,768]{1,0:T(8,128)} %get-tuple-element.149, f32[128]{0:T(128)S(1)} %broadcast_add_fusion, f32[128,768]{1,0:T(8,128)} %get-tuple-element.148, bf16[128,768]{1,0:T(8,128)(2,1)S(1)} %copy-done.1), kind=kLoop, calls=%fused_computation.15 | loop fusion | flops 688128 | bytes 1376768 | tf_op jit(solution)/shard_map/convert_element_type | solution.py:88
  (38 shorter events, 0.5 us)
Async XLA Ops:
  7.2 45.4 %all-gather.4.cloned.1.call-start = ((), (), s32[]{:S(2)}) async-start(), calls=%async_computation | async-start | bytes 1671168 | tf_op jit(solution)/shard_map/all_gather | solution.py:79
  7.9 120.3 %all-reduce.3.cloned.1.call-start = ((), (), s32[]{:S(2)}) async-start(), calls=%async_computation.1 | async-start | bytes 1572864 | tf_op jit(solution)/shard_map/psum | solution.py:85
  54.7 38.3 %copy-start = (bf16[1024,768]{1,0:T(8,128)(2,1)S(1)}, bf16[1024,768]{1,0:T(8,128)(2,1)}, u32[]{:S(2)}) copy-start(bf16[1024,768]{1,0:T(8,128)(2,1)} %all-gather.4.cloned.1.call-done) | copy-start | bytes 4718596
  94.2 34.0 %copy-start.1 = (bf16[128,768]{1,0:T(8,128)(2,1)S(1)}, bf16[128,768]{1,0:T(8,128)(2,1)}, u32[]{:S(2)}) copy-start(bf16[128,768]{1,0:T(8,128)(2,1)} %param.6) | copy-start | bytes 589828
Sparse Core Ops, SparseCore 0:
  10.3 42.3 all-gather.3
  95.5 32.7 all-reduce.2
where the time goes:
time: 137 us
  waiting for transfers between devices  71 us (52%)
  blocking collectives  42 us (31%)
  between operations  14.7 us (11%)
  matrix products  4.43 us (3%)
  other arithmetic  4.09 us (3%)
    all_gather x1, waiting for transfers between devices, shards(): row_piece = lax.all_gather(embeddings, 'cent', axis=0, tiled=True)  43 us
    all_gather x2, blocking collectives, combined_all(): gathered = jax.tree.map(lambda a: lax.all_gather(a, axis), part)  37 us
    psum x1, waiting for transfers between devices, shards(): lax.psum((weighted, moments, weight_mass), 'rows')  27.3 us
    psum x1, blocking collectives, shards(): lax.psum((weighted, moments, weight_mass), 'rows')  4.93 us
  transfers between devices with their start and end apart: 2, of which 2 were waited for; matrix products, arithmetic and copies ran while one was open for 1% of the time, Pallas kernels for 0%

commit v1 on v0

--- a/solution.py
+++ b/solution.py
@@ -76,7 +76,9 @@
     exp_sums = piece_total
     peaks, exp_sums = (peaks, exp_sums)
     group_lse = finish_totals(peaks, exp_sums)
-    row_piece = lax.all_gather(embeddings, "cent", axis=0, tiled=True)
+    row_piece = jnp.concatenate(
+        lax.all_to_all(jnp.stack([embeddings] * lax.axis_size("cent")), "cent", 0, 0), axis=0
+    )
     piece_count = row_piece.shape[0]
     logits = scores(row_piece, centroids, squared_norm, factor)
     positions = jnp.arange(piece_count, dtype=jnp.int32)

time: 137 us -> 155 us (1.13)
  starting transfers between devices: 0.08 us -> 7.62 us
  waiting for transfers between devices: 71 us -> 77.6 us
  local copies, waits for them, and re-layouts: 0.27 us -> 2.46 us
    all_to_all x0 -> x1, starting transfers between devices: none -> 7.55 us  [shards(): lax.all_to_all(jnp.stack([embeddings] * lax.axis_size('cent')), 'cent', 0...]
    all_gather x1, waiting for transfers between devices: 43 us -> 49.5 us  [shards(): lax.all_gather(embeddings, 'cent', axis=0, tiled=True)]
    another operation x0 -> x1, local copies, waits for them, and re-layouts: none -> 2.2 us  [shards(): jnp.stack([embeddings] * lax.axis_size('cent'))]
  transfers between devices with their start and end apart: 2 -> 3, of which waited for: 2 -> 2; matrix products, arithmetic and copies ran while one was open for 1% -> 4% of each run, Pallas kernels for 0% -> 0%
where the time goes in v1:
time: 155 us
  waiting for transfers between devices  77.6 us (50%)
  blocking collectives  43.4 us (28%)
  between operations  14.8 us (10%)
  starting transfers between devices  7.62 us (5%)
  matrix products  5.02 us (3%)
  other arithmetic  3.27 us (2%)
  local copies, waits for them, and re-layouts  2.46 us (2%)
    all_gather x1, waiting for transfers between devices, shards(): lax.all_gather(embeddings, 'cent', axis=0, tiled=True)  49.5 us
    all_gather x2, blocking collectives, combined_all(): gathered = jax.tree.map(lambda a: lax.all_gather(a, axis), part)  38.5 us
    psum x1, waiting for transfers between devices, shards(): lax.psum((weighted, moments, weight_mass), 'rows')  27.4 us
    all_to_all x1, starting transfers between devices, shards(): lax.all_to_all(jnp.stack([embeddings] * lax.axis_size('cent')), 'cent', 0...  7.55 us
    psum x1, blocking collectives, shards(): lax.psum((weighted, moments, weight_mass), 'rows')  4.93 us
  transfers between devices with their start and end apart: 3, of which 2 were waited for; matrix products, arithmetic and copies ran while one was open for 4% of the time, Pallas kernels for 0%

profile of v1, /device:TPU:0, one launch (start us, length us, event | category | flops | bytes accessed | tf_op | source)
XLA Modules:
  0.0 154.6 jit_solution(13595821174738202462)
XLA Ops:
  7.2 0.0 all-gather.4.cloned.1.call-start
  7.2 0.7 all-gather.4.cloned.1.call-update
  7.9 2.2 %stack.2 = bf16[16,64,768]{2,1,0:T(8,128)(2,1)} broadcast(bf16[64,768]{1,0:T(8,128)(2,1)} %param.5), dimensions={1,2} | broadcast | bytes 1671168 | tf_op jit(solution)/shard_map/stack | solution.py:80
  10.1 0.0 copy-start
  10.1 7.5 %all-to-all-start = ((bf16[16,64,768]{2,1,0:T(8,128)(2,1)}), bf16[16,64,768]{2,1,0:T(8,128)(2,1)S(1)}, u32[]{:S(2)}, u32[]{:S(2)}) async-start(bf16[16,64,768]{2,1,0:T(8,128)(2,1)} %stack.2), calls=%async_computation | async-start | bytes 3145728 | tf_op jit(solution)/shard_map/all_to_all | solution.py:80
  17.6 0.0 all-reduce.3.cloned.1.call-start
  18.4 0.0 copy-done
  18.4 0.1 fusion.7
  18.5 49.5 %all-gather.4.cloned.1.call-done = bf16[1024,768]{1,0:T(8,128)(2,1)} async-done(((bf16[64,768]{1,0:T(8,128)(2,1)}), bf16[1024,768]{1,0:T(8,128)(2,1)}) %all-gather.4.cloned.1.call-update) | async-done | bytes 1572880 | tf_op jit(solution)/shard_map/all_gather | solution.py:71
  68.0 2.1 %fusion.10 = (f32[1024]{0:T(1024)S(1)}, f32[1024,128]{1,0:T(8,128)S(1)}) fusion(f32[128]{0:T(128)S(1)} %broadcast_multiply_fusion, bf16[1024,768]{1,0:T(8,128)(2,1)} %all-gather.4.cloned.1.call-done, bf16[128,768]{1,0:T(8,128)(2,1)S(1)} %copy-done), kind=kOutput, calls=%fused_computation.26 | convolution fusion | flops 201718784 | bytes 2298368 | tf_op jit(solution)/shard_map/dot_general | solution.py:25
  70.0 0.4 exponential_reduce_fusion
  70.4 20.9 %all-gather.1 = f32[16384]{0:T(1024)S(1)} all-gather(f32[1024]{0:T(1024)S(1)} %exponential_reduce_fusion), channel_id=3, replica_groups=mesh['rows'=2,'cent'=16] {'cent'}, dimensions={0}, use_global_device_ids=true | all-gather | bytes 69632 | tf_op jit(solution)/shard_map/all_gather | solution.py:14
  91.3 17.6 %all-gather = f32[16384]{0:T(1024)S(1)} all-gather(f32[1024]{0:T(1024)S(1)} %get-tuple-element.156), channel_id=2, replica_groups=mesh['rows'=2,'cent'=16] {'cent'}, dimensions={0}, use_global_device_ids=true | all-gather | bytes 69632 | tf_op jit(solution)/shard_map/all_gather | solution.py:14
  108.9 0.9 while.17
  109.9 0.0 all-to-all-done
  109.9 0.6 convert_reduce_fusion
  110.5 1.2 fusion
  111.7 1.2 fusion.11
  112.8 0.0 all-reduce.3.cloned.1.call-update
  112.9 4.9 %psum.22 = f32[128]{0:T(128)S(1)} all-reduce(f32[128]{0:T(128)S(1)} %get-tuple-element.158), channel_id=1, replica_groups=mesh['rows'=2,'cent'=16] {'rows'}, use_global_device_ids=true, to_apply=%region_7.8 | all-reduce | flops 128 | bytes 1024 | tf_op jit(solution)/shard_map/psum | solution.py:87
  117.8 0.6 compare_select_fusion
  118.4 27.4 %all-reduce.3.cloned.1.call-done = (f32[128,768]{1,0:T(8,128)}, f32[128,768]{1,0:T(8,128)}) async-done(((f32[128,768]{1,0:T(8,128)}, f32[128,768]{1,0:T(8,128)}), (f32[128,768]{1,0:T(8,128)}, f32[128,768]{1,0:T(8,128)})) %all-reduce.3.cloned.1.call-update) | async-done | bytes 786448 | tf_op jit(solution)/shard_map/psum | solution.py:87
  145.8 2.0 %divide_convert_fusion = (bf16[128,768]{1,0:T(8,128)(2,1)}, bf16[128,768]{1,0:T(8,128)(2,1)}) fusion(f32[128,768]{1,0:T(8,128)} %get-tuple-element.149, f32[128]{0:T(128)S(1)} %broadcast_add_fusion, f32[128,768]{1,0:T(8,128)} %get-tuple-element.148, bf16[128,768]{1,0:T(8,128)(2,1)S(1)} %copy-done), kind=kLoop, calls=%fused_computation.20 | loop fusion | flops 688128 | bytes 1376768 | tf_op jit(solution)/shard_map/convert_element_type | solution.py:90
  (38 shorter events, 0.5 us)
Async XLA Ops:
  7.2 60.8 %all-gather.4.cloned.1.call-start = ((), (), s32[]{:S(2)}) async-start(), calls=%async_computation.1 | async-start | bytes 1671168 | tf_op jit(solution)/shard_map/all_gather | solution.py:71
  10.1 8.3 %copy-start = (bf16[128,768]{1,0:T(8,128)(2,1)S(1)}, bf16[128,768]{1,0:T(8,128)(2,1)}, u32[]{:S(2)}) copy-start(bf16[128,768]{1,0:T(8,128)(2,1)} %param.6) | copy-start | bytes 589828
  10.1 99.8 %all-to-all-start = ((bf16[16,64,768]{2,1,0:T(8,128)(2,1)}), bf16[16,64,768]{2,1,0:T(8,128)(2,1)S(1)}, u32[]{:S(2)}, u32[]{:S(2)}) async-start(bf16[16,64,768]{2,1,0:T(8,128)(2,1)} %stack.2), calls=%async_computation | async-start | bytes 3145728 | tf_op jit(solution)/shard_map/all_to_all | solution.py:80
  17.6 128.1 %all-reduce.3.cloned.1.call-start = ((), (), s32[]{:S(2)}) async-start(), calls=%async_computation.2 | async-start | bytes 1572864 | tf_op jit(solution)/shard_map/psum | solution.py:87
Sparse Core Ops, SparseCore 0:
  10.3 57.6 all-gather.3
  113.0 32.7 all-reduce.2
